TPU v7x, 32 devices: a whole 2x2x4 slice. The times are simulated.
32 devices in a mesh: fsdp: 2 (over x), ctx: 4 (over z), tp: 4 (over y, core).
Axes of the slice: x: 2, y: 2, z: 4, core: 2. Of those that a mesh axis runs over, the one named last changes fastest.
Arguments:
- tokens: bfloat16 [4, 1024, 2048], P('fsdp', 'ctx'), may hold values from -36 to 36
- cotangent: bfloat16 [4, 1024, 2048], P('fsdp', 'ctx'), may hold values from -9 to 9
- lengths: int32 [4, 2], P('fsdp'), may hold values from 1 to 768, 1024 in all within a row
- deal: int32 [4, 1024], P('fsdp'), may hold values from 0 to 1023, each once within a row
- att_proj: float32 [3, 2048, 2048], P(None, ('fsdp', 'ctx'), 'tp'), may hold values from -0.125 to 0.125
- attn_out: float32 [2048, 2048], P(('fsdp', 'ctx'), 'tp'), may hold values from -0.75 to 0.75
- ff_proj: float32 [2, 2048, 8192], P(None, ('fsdp', 'ctx'), 'tp'), may hold values from -0.125 to 0.125
- ff_out: float32 [2048, 8192], P(('fsdp', 'ctx'), 'tp'), may hold values from -0.0625 to 0.0625
- att_proj_first: float32 [3, 2048, 2048], P(None, ('fsdp', 'ctx'), 'tp')
- attn_out_first: float32 [2048, 2048], P(('fsdp', 'ctx'), 'tp')
- ff_proj_first: float32 [2, 2048, 8192], P(None, ('fsdp', 'ctx'), 'tp')
- ff_out_first: float32 [2048, 8192], P(('fsdp', 'ctx'), 'tp')
- att_proj_second: float32 [3, 2048, 2048], P(None, ('fsdp', 'ctx'), 'tp'), as said below
- attn_out_second: float32 [2048, 2048], P(('fsdp', 'ctx'), 'tp'), as said below
- ff_proj_second: float32 [2, 2048, 8192], P(None, ('fsdp', 'ctx'), 'tp'), as said below
- ff_out_second: float32 [2048, 8192], P(('fsdp', 'ctx'), 'tp'), as said below
Outputs:
- block_out: bfloat16 [4, 1024, 2048], P('fsdp', 'ctx')
- input_grad: float32 [4, 1024, 2048], P('fsdp', 'ctx')
- grad_norm: float32 [1], replicated
- att_proj_grad: float32 [3, 2048, 2048], P(None, ('fsdp', 'ctx'), 'tp')
- attn_out_grad: float32 [2048, 2048], P(('fsdp', 'ctx'), 'tp')
- ff_proj_grad: float32 [2, 2048, 8192], P(None, ('fsdp', 'ctx'), 'tp')
- ff_out_grad: float32 [2048, 8192], P(('fsdp', 'ctx'), 'tp')
- att_proj_first_new: float32 [3, 2048, 2048], P(None, ('fsdp', 'ctx'), 'tp')
- attn_out_first_new: float32 [2048, 2048], P(('fsdp', 'ctx'), 'tp')
- ff_proj_first_new: float32 [2, 2048, 8192], P(None, ('fsdp', 'ctx'), 'tp')
- ff_out_first_new: float32 [2048, 8192], P(('fsdp', 'ctx'), 'tp')
- att_proj_second_new: float32 [3, 2048, 2048], P(None, ('fsdp', 'ctx'), 'tp')
- attn_out_second_new: float32 [2048, 2048], P(('fsdp', 'ctx'), 'tp')
- ff_proj_second_new: float32 [2, 2048, 8192], P(None, ('fsdp', 'ctx'), 'tp')
- ff_out_second_new: float32 [2048, 8192], P(('fsdp', 'ctx'), 'tp')
- att_proj_new: float32 [3, 2048, 2048], P(None, ('fsdp', 'ctx'), 'tp')
- attn_out_new: float32 [2048, 2048], P(('fsdp', 'ctx'), 'tp')
- ff_proj_new: float32 [2, 2048, 8192], P(None, ('fsdp', 'ctx'), 'tp')
- ff_out_new: float32 [2048, 8192], P(('fsdp', 'ctx'), 'tp')
- att_proj_low: bfloat16 [3, 2048, 2048], P(None, ('fsdp', 'ctx'), 'tp')
- attn_out_low: bfloat16 [2048, 2048], P(('fsdp', 'ctx'), 'tp')
- ff_proj_low: bfloat16 [2, 2048, 8192], P(None, ('fsdp', 'ctx'), 'tp')
- ff_out_low: bfloat16 [2048, 8192], P(('fsdp', 'ctx'), 'tp')
Inputs may be any that keep to these rules, and one draw needn't show every extreme that they name: `lengths`: each row sums to 1024 and no entry exceeds 768. `deal`: each row is a permutation of the positions of its pack. `att_proj_second`: every entry is positive. `attn_out_second`: every entry is positive. `ff_proj_second`: every entry is positive. `ff_out_second`: every entry is positive.
All inputs are finite; a program needn't handle non-finite values.
Results may differ from a plain program's by a relative error of at most 0.017.
Values may be sent and summed in bfloat16 or wider, within the bound.
A program may use at most 320 MiB of HBM per device.

v0:
```python
import jax
import jax.numpy as jnp
from jax import lax
from jax.sharding import PartitionSpec as P

HEAD_DIM = 128
STEP = 10
EPS_NORM = 1e-05
BETA_ONE = 0.9
BETA_TWO = 0.95
EPS_ADAM = 1e-08
DECAY = 0.1
MAX_NORM = 1.0
NEG_FILL = -1e30
BF = jnp.bfloat16
F32 = jnp.float32


def mean_spread(values):
    centre = values - jnp.mean(values, axis=-1, keepdims=True)
    spread = jnp.mean(centre * centre, axis=-1, keepdims=True)
    scale = lax.rsqrt(spread + EPS_NORM)
    return (centre * scale, scale)


def norm_back(grad, normed, scale):
    return scale * (
        grad
        - jnp.mean(grad, axis=-1, keepdims=True)
        - normed * jnp.mean(grad * normed, axis=-1, keepdims=True)
    )


def dot(left, right, dims):
    return lax.dot_general(left, right, (dims, ((), ())), preferred_element_type=F32)


def adam_step(weight, grad_sum, first, second, clip_factor, learn_rate):
    clipped = grad_sum * clip_factor
    first_new = BETA_ONE * first + (1.0 - BETA_ONE) * clipped
    second_new = BETA_TWO * second + (1.0 - BETA_TWO) * clipped * clipped
    first_hat = first_new / (1.0 - BETA_ONE**STEP)
    second_hat = second_new / (1.0 - BETA_TWO**STEP)
    weight_new = weight - learn_rate * (
        first_hat / (jnp.sqrt(second_hat) + EPS_ADAM) + DECAY * weight
    )
    return (first_new, second_new, weight_new)


def make_shards(mesh):
    n_f, n_c, n_t = (mesh.shape[a] for a in ("fsdp", "ctx", "tp"))

    def by_ctx(block, shift):
        return lax.ppermute(block, "ctx", [(i, (i + shift) % n_c) for i in range(n_c)])

    def by_core(block):
        return lax.ppermute(block, "tp", [(i, i ^ 1) for i in range(n_t)])

    def by_pack(block, shift, other):
        pairs = [
            (f * n_t + t, (f + shift) % n_f * n_t + (t ^ 2 * other))
            for f in range(n_f)
            for t in range(n_t)
        ]
        return lax.ppermute(block, ("fsdp", "tp"), pairs)

    def gather_rows(half):
        mine = jnp.stack([half] + [by_ctx(half, s) for s in range(1, n_c)])
        both = jnp.stack([mine, by_core(mine)], axis=1)
        return both.reshape(-1, half.shape[1])

    def scatter_rows(partial):
        width = partial.shape[1]
        split = partial.astype(BF).reshape(n_c, 2, -1, width)
        summed = split[:, 0].astype(F32) + by_core(split[:, 1]).astype(F32)
        sent = summed.astype(BF)
        total = summed[0]
        for j in range(1, n_c):
            total = total + by_ctx(sent[j], -j).astype(F32)
        return total

    def gather_weight(shard):
        swapped = lax.all_to_all(shard.astype(BF), "ctx", 2, 1, tiled=True)
        columns = []
        for other in range(2):
            parts = [
                swapped if s == 0 and other == 0 else by_pack(swapped, s, other) for s in range(n_f)
            ]
            columns.append(jnp.concatenate(parts, axis=1))
        return jnp.concatenate(columns, axis=2)

    def scatter_grad(grad):
        count, height, width = grad.shape
        low = grad.astype(BF).reshape(count, n_f, height // n_f, 2, width // 2)
        total = grad.reshape(low.shape)[:, 0, :, 0]
        for other in range(2):
            for i in range(n_f):
                if i or other:
                    total = total + by_pack(low[:, i, :, other], -i, other).astype(F32)
        return lax.all_to_all(total.astype(BF), "ctx", 1, 2, tiled=True).astype(F32)

    def shards(
        tokens,
        cotangent,
        lengths,
        deal,
        att_proj,
        attn_out,
        ff_proj,
        ff_out,
        att_proj_first,
        attn_out_first,
        ff_proj_first,
        ff_out_first,
        att_proj_second,
        attn_out_second,
        ff_proj_second,
        ff_out_second,
    ):
        f_at, c_at, t_at = (lax.axis_index(a) for a in ("fsdp", "ctx", "tp"))
        pack_at, core_at = (t_at // 2, t_at % 2)
        packs, row_count, width = tokens.shape
        half = row_count // 2
        pack_len = deal.shape[1]
        score_scale = HEAD_DIM ** (-0.5)
        f_width = width // n_f

        def turned(rows):
            return jnp.concatenate(
                [
                    lax.dynamic_slice_in_dim(rows, (f_at - i) % n_f * f_width, f_width, 1)
                    for i in range(n_f)
                ],
                axis=1,
            )

        def own_rows(array):
            rows = array.reshape(packs * 2, half, width)
            return turned(lax.dynamic_index_in_dim(rows, t_at, 0, keepdims=False))

        own_tokens = own_rows(tokens)
        own_cot = own_rows(cotangent)
        att_w = gather_weight(jnp.concatenate([att_proj, attn_out[None]]))
        own_input = own_tokens.astype(F32)
        normed_one, scale_one = mean_spread(own_input)
        act_one = gather_rows(normed_one.astype(BF))
        deal_pack = lax.dynamic_index_in_dim(deal, pack_at, 0, keepdims=False)
        length_row = lax.dynamic_index_in_dim(lengths, pack_at, 0, keepdims=False)
        places = jnp.concatenate(
            [
                lax.dynamic_slice_in_dim(
                    deal_pack, (c_at - j) % n_c * row_count + (core_at + h) % 2 * half, half
                )
                for j in range(n_c)
                for h in range(2)
            ]
        )
        seqs = lengths.shape[1]
        before = jnp.arange(seqs)[:, None] > jnp.arange(seqs)[None, :]
        starts = jnp.sum(jnp.where(before, length_row[None, :], 0), axis=1)
        inside = (places[:, None] >= starts[None, :]) & (
            places[:, None] < (starts + length_row)[None, :]
        )
        firsts = jnp.sum(jnp.where(inside, starts[None, :], 0), axis=1)
        allowed = (places[None, :] <= places[:, None]) & (places[None, :] >= firsts[:, None])
        freq_steps = jnp.arange(HEAD_DIM // 2, dtype=F32)
        inverse = jnp.power(10000.0, -2.0 * freq_steps / HEAD_DIM)
        angles = (places - firsts).astype(F32)[:, None] * inverse[None, :]
        cos_table, sine_table = (jnp.cos(angles), jnp.sin(angles))

        def turn(values, sign):
            low, high = (values[..., : HEAD_DIM // 2], values[..., HEAD_DIM // 2 :])
            sine = sign * sine_table[:, None, :]
            cos = cos_table[:, None, :]
            return jnp.concatenate([low * cos - high * sine, high * cos + low * sine], axis=-1)

        rank_width = att_w.shape[2]
        heads = rank_width // HEAD_DIM
        raw = [
            dot(act_one, att_w[i], ((1,), (0,))).reshape(pack_len, heads, HEAD_DIM)
            for i in range(3)
        ]
        query = turn(raw[0], 1.0).astype(BF)
        key = turn(raw[1], 1.0).astype(BF)
        value = raw[2].astype(BF)
        scores = jnp.einsum("thd,khd->htk", query, key, preferred_element_type=F32) * score_scale
        scores = jnp.where(allowed[None], scores, NEG_FILL)
        exp_scores = jnp.exp(scores - jnp.max(scores, axis=2, keepdims=True))
        probs = exp_scores / jnp.sum(exp_scores, axis=2, keepdims=True)
        probs_low = probs.astype(BF)
        attended = jnp.einsum("htk,khd->thd", probs_low, value, preferred_element_type=F32)
        attended_low = attended.reshape(pack_len, rank_width).astype(BF)
        out_part = dot(attended_low, att_w[3], ((1,), (1,)))
        resid_mid = own_input + scatter_rows(out_part)
        normed_two, scale_two = mean_spread(resid_mid)
        act_two = gather_rows(normed_two.astype(BF))
        ff_w = gather_weight(jnp.concatenate([ff_proj, ff_out[None]]))
        cot_rows = gather_rows(own_cot)
        up = dot(act_two, ff_w[0], ((1,), (0,)))
        gate = dot(act_two, ff_w[1], ((1,), (0,)))
        sigma = jax.nn.sigmoid(gate)
        hidden_low = (gate * sigma * up).astype(BF)
        hidden_grad = dot(cot_rows, ff_w[2], ((1,), (0,)))
        up_grad = (hidden_grad * gate * sigma).astype(BF)
        gate_grad = (hidden_grad * up * sigma * (1.0 + gate * (1.0 - sigma))).astype(BF)
        act_two_part = dot(up_grad, ff_w[0], ((1,), (1,))) + dot(gate_grad, ff_w[1], ((1,), (1,)))
        act_two_grad = scatter_rows(act_two_part)
        mid_grad = own_cot.astype(F32) + norm_back(act_two_grad, normed_two, scale_two)
        mid_rows = gather_rows(mid_grad.astype(BF))
        ff_branch = scatter_rows(dot(hidden_low, ff_w[2], ((1,), (1,))))
        block_rows = turned((resid_mid + ff_branch).astype(BF))
        block_out = lax.all_gather(block_rows, "tp", axis=0, tiled=True)
        ff_grad = jnp.stack(
            [
                dot(act_two, up_grad, ((0,), (0,))),
                dot(act_two, gate_grad, ((0,), (0,))),
                dot(cot_rows, hidden_low, ((0,), (0,))),
            ]
        )
        ff_total = scatter_grad(ff_grad)
        attended_grad = dot(mid_rows, att_w[3], ((1,), (0,))).astype(BF)
        attended_grad = attended_grad.reshape(pack_len, heads, HEAD_DIM)
        value_grad = jnp.einsum(
            "htk,thd->khd", probs_low, attended_grad, preferred_element_type=F32
        )
        prob_grad = jnp.einsum("thd,khd->htk", attended_grad, value, preferred_element_type=F32)
        delta_rows = jnp.sum(probs * prob_grad, axis=2, keepdims=True)
        score_grad = (probs * (prob_grad - delta_rows)).astype(BF)
        query_grad = (
            jnp.einsum("htk,khd->thd", score_grad, key, preferred_element_type=F32) * score_scale
        )
        key_grad = (
            jnp.einsum("htk,thd->khd", score_grad, query, preferred_element_type=F32) * score_scale
        )
        joint_grad = [
            part.reshape(pack_len, rank_width).astype(BF)
            for part in (turn(query_grad, -1.0), turn(key_grad, -1.0), value_grad)
        ]
        act_one_part = sum((dot(joint_grad[i], att_w[i], ((1,), (1,))) for i in range(3)))
        act_one_grad = scatter_rows(act_one_part)
        input_rows = turned(norm_back(act_one_grad, normed_one, scale_one) + mid_grad)
        input_grad = lax.all_gather(input_rows, "tp", axis=0, tiled=True)
        att_grad = jnp.stack(
            [dot(act_one, part, ((0,), (0,))) for part in joint_grad]
            + [dot(mid_rows, attended_low, ((0,), (0,)))]
        )
        att_total = scatter_grad(att_grad)
        square_sum = lax.psum(
            jnp.sum(att_total * att_total) + jnp.sum(ff_total * ff_total), ("fsdp", "ctx", "tp")
        )
        norm_value = jnp.sqrt(square_sum)
        clip_factor = jnp.minimum(1.0, MAX_NORM / (norm_value + 1e-06))
        base_rate = width ** (-0.5)
        out_rate = (width // 32) ** (-0.5)
        grads = (att_total[:3], att_total[3], ff_total[:2], ff_total[2])
        weights = (att_proj, attn_out, ff_proj, ff_out)
        firsts_old = (att_proj_first, attn_out_first, ff_proj_first, ff_out_first)
        seconds_old = (att_proj_second, attn_out_second, ff_proj_second, ff_out_second)
        rates = (base_rate, out_rate, base_rate, base_rate)
        news = [
            adam_step(w, g, m, v, clip_factor, r)
            for w, g, m, v, r in zip(weights, grads, firsts_old, seconds_old, rates)
        ]
        return (
            block_out.reshape(tokens.shape),
            input_grad.reshape(tokens.shape),
            norm_value.reshape(1),
            *grads,
            *(n[0] for n in news),
            *(n[1] for n in news),
            *(n[2] for n in news),
            *(n[2].astype(BF) for n in news),
        )

    return shards


def solution(mesh):
    act = P("fsdp", "ctx", None)
    table = P("fsdp", None)
    cube = P(None, ("fsdp", "ctx"), "tp")
    flat = P(("fsdp", "ctx"), "tp")
    group = (cube, flat, cube, flat)
    in_specs = (act, act, table, table) + group * 3
    out_specs = (act, act, P()) + group * 5
    return jax.shard_map(
        make_shards(mesh), mesh=mesh, in_specs=in_specs, out_specs=out_specs, check_vma=False
    )
```

profile of v0, /device:TPU:0, one launch (start us, length us, event | category | flops | bytes accessed | tf_op | source)
XLA Modules:
  0.0 1239.6 jit_solution(7783477940593059198)
XLA Ops:
  28.0 44.8 %collective-permute-done.1 = bf16[128,2048]{1,0:T(8,128)(2,1)} collective-permute-done((bf16[128,2048]{1,0:T(8,128)(2,1)}, bf16[128,2048]{1,0:T(8,128)(2,1)}, u32[]{:S(2)}, u32[]{:S(2)}) %collective-permute-start.1) | collective-permute-done | bytes 524320 | tf_op jit(solution)/shard_map/ppermute | solution.py:54
  93.8 17.7 %collective-permute-done.6 = bf16[4,1024,128]{1,2,0:T(8,128)(2,1)S(1)} collective-permute-done((bf16[4,1024,128]{1,2,0:T(8,128)(2,1)S(1)}, bf16[4,1024,128]{1,2,0:T(8,128)(2,1)S(1)}, u32[]{:S(2)}, u32[]{:S(2)}) %collective-permute-start.6) | collective-permute-done | bytes 1048608 | tf_op jit(solution)/shard_map/ppermute | solution.py:65
  111.4 20.4 %collective-permute-done.5 = bf16[4,1024,128]{1,2,0:T(8,128)(2,1)S(1)} collective-permute-done((bf16[4,1024,128]{1,2,0:T(8,128)(2,1)S(1)}, bf16[4,1024,128]{1,2,0:T(8,128)(2,1)S(1)}, u32[]{:S(2)}, u32[]{:S(2)}) %collective-permute-start.5) | collective-permute-done | bytes 1048608 | tf_op jit(solution)/shard_map/ppermute | solution.py:65
  189.7 71.6 %collective-permute-done.10 = bf16[128,2048]{1,0:T(8,128)(2,1)S(1)} collective-permute-done((bf16[128,2048]{1,0:T(8,128)(2,1)S(1)}, bf16[128,2048]{1,0:T(8,128)(2,1)S(1)}, u32[]{:S(2)}, u32[]{:S(2)}) %collective-permute-start.10) | collective-permute-done | bytes 524320 | tf_op jit(solution)/shard_map/ppermute | solution.py:54
  261.3 65.1 %collective-permute-start.22 = (bf16[128,2048]{1,0:T(8,128)(2,1)S(1)}, bf16[128,2048]{1,0:T(8,128)(2,1)S(1)}, u32[]{:S(2)}, u32[]{:S(2)}) collective-permute-start(bf16[128,2048]{1,0:T(8,128)(2,1)S(1)} %get-tuple-element.108), channel_id=1, source_target_pairs={{0,4},{4,8},{8,12},{12,0},{1,5},{5,9},{9,13},{13,1},{2,6},{6,10},{... | collective-permute-start | bytes 1572872 | tf_op jit(solution)/shard_map/ppermute | solution.py:54
  329.5 12.8 %collective-permute-start.13 = (bf16[128,2048]{1,0:T(8,128)(2,1)}, bf16[128,2048]{1,0:T(8,128)(2,1)}, u32[]{:S(2)}, u32[]{:S(2)}) collective-permute-start(bf16[128,2048]{1,0:T(8,128)(2,1)} %fusion.76), channel_id=1, source_target_pairs={{0,12},{4,0},{8,4},{12,8},{1,13},{5,1},{9,5},{13,9},{2,14},{6,2},{... | collective-permute-start | bytes 1572872 | tf_op jit(solution)/shard_map/ppermute | solution.py:54
  350.8 33.1 %collective-permute-done.23 = bf16[128,2048]{1,0:T(8,128)(2,1)S(1)} collective-permute-done((bf16[128,2048]{1,0:T(8,128)(2,1)S(1)}, bf16[128,2048]{1,0:T(8,128)(2,1)S(1)}, u32[]{:S(2)}, u32[]{:S(2)}) %collective-permute-start.23) | collective-permute-done | bytes 524320 | tf_op jit(solution)/shard_map/ppermute | solution.py:54
  423.3 11.2 copy.390
  451.4 15.5 %collective-permute-done.17 = bf16[3,1024,512]{2,1,0:T(8,128)(2,1)} collective-permute-done((bf16[3,1024,512]{2,1,0:T(8,128)(2,1)}, bf16[3,1024,512]{2,1,0:T(8,128)(2,1)}, u32[]{:S(2)}, u32[]{:S(2)}) %collective-permute-start.17) | collective-permute-done | bytes 3145760 | tf_op jit(solution)/shard_map/ppermute | solution.py:65
  466.9 67.0 %collective-permute-done.16 = bf16[3,1024,512]{2,1,0:T(8,128)(2,1)} collective-permute-done((bf16[3,1024,512]{2,1,0:T(8,128)(2,1)}, bf16[3,1024,512]{2,1,0:T(8,128)(2,1)}, u32[]{:S(2)}, u32[]{:S(2)}) %collective-permute-start.16) | collective-permute-done | bytes 3145760 | tf_op jit(solution)/shard_map/ppermute | solution.py:65
  533.8 14.6 %maximum_maximum_fusion = bf16[3,2048,1024]{2,1,0:T(8,128)(2,1)S(1)} fusion(bf16[3,1024,512]{2,1,0:T(8,128)(2,1)} %collective-permute-done.17, bf16[3,1024,512]{2,1,0:T(8,128)(2,1)} %collective-permute-done.16, bf16[3,1024,512]{2,1,0:T(8,128)(2,1)} %collective-permute-done.15, bf16[3,1024,512]{2,1,0:T(8,128)(2,1)} %bitcast.502), kind=kLoop, calls=%fused_computation.2 | loop fusion | flops 50331648 | bytes 25165824 | tf_op jit(solution)/shard_map/concatenate | solution.py:90
  566.9 14.0 %fusion.12 = (bf16[1024,1024]{1,0:T(8,128)(2,1)}, bf16[1024,1024]{1,0:T(8,128)(2,1)}, bf16[1024,1024]{1,0:T(8,128)(2,1)}, f32[1024,1024]{0,1:T(8,128)}) fusion(f32[1024,1024]{0,1:T(8,128)} %fusion.23, f32[1024,1024]{0,1:T(8,128)} %fusion.22, bf16[1024,2048]{1,0:T(8,128)(2,1)} %bitcast.482, bf16[3,2048,1024]{2,1,0:T(8,128)(2,1)} %copy-done.14), kind=kOutput, calls=%fused_computation.43 | convolution fusion | flops 4311744512 | bytes 27262976 | tf_op jit(solution)/shard_map/dot_general | solution.py:35
  611.3 11.6 add_convert_fusion.1
  659.7 22.3 %collective-permute-done.28 = bf16[128,2048]{1,0:T(8,128)(2,1)} collective-permute-done((bf16[128,2048]{1,0:T(8,128)(2,1)}, bf16[128,2048]{1,0:T(8,128)(2,1)}, u32[]{:S(2)}, u32[]{:S(2)}) %collective-permute-start.28) | collective-permute-done | bytes 524320 | tf_op jit(solution)/shard_map/ppermute | solution.py:54
  693.4 32.7 %collective-permute-done.20 = bf16[128,2048]{1,0:T(8,128)(2,1)S(1)} collective-permute-done((bf16[128,2048]{1,0:T(8,128)(2,1)S(1)}, bf16[128,2048]{1,0:T(8,128)(2,1)S(1)}, u32[]{:S(2)}, u32[]{:S(2)}) %collective-permute-start.20) | collective-permute-done | bytes 524320 | tf_op jit(solution)/shard_map/ppermute | solution.py:54
  726.9 11.0 collective-permute-start.32
  750.4 33.8 %collective-permute-done.31 = bf16[128,2048]{1,0:T(8,128)(2,1)S(1)} collective-permute-done((bf16[128,2048]{1,0:T(8,128)(2,1)S(1)}, bf16[128,2048]{1,0:T(8,128)(2,1)S(1)}, u32[]{:S(2)}, u32[]{:S(2)}) %collective-permute-start.31) | collective-permute-done | bytes 524320 | tf_op jit(solution)/shard_map/ppermute | solution.py:54
  799.4 12.5 %pad_maximum_fusion = f32[3,2,1024,2,512]{4,2,3,1,0:T(8,128)} fusion(f32[1,2,1024,2,512]{4,2,3,1,0:T(8,128)} %convolution_bitcast_fusion, f32[1,2,1024,2,512]{4,2,3,1,0:T(8,128)S(1)} %convolution_bitcast_fusion.1, f32[1,2,1024,2,512]{4,2,3,1,0:T(8,128)S(1)} %convolution_bitcast_fusion.2), kind=kLoop, calls=%fused_computation.1 | loop fusion | flops 12582912 | bytes 50331648 | tf_op jit(solution)/shard_map/stack | solution.py:213
  845.0 23.0 %collective-permute-done.43 = bf16[3,1024,512]{2,1,0:T(8,128)(2,1)} collective-permute-done((bf16[3,1024,512]{2,1,0:T(8,128)(2,1)}, bf16[3,1024,512]{2,1,0:T(8,128)(2,1)}, u32[]{:S(2)}, u32[]{:S(2)}) %collective-permute-start.43) | collective-permute-done | bytes 3145760 | tf_op jit(solution)/shard_map/ppermute | solution.py:65
  868.1 78.2 %collective-permute-done.42 = bf16[3,1024,512]{2,1,0:T(8,128)(2,1)} collective-permute-done((bf16[3,1024,512]{2,1,0:T(8,128)(2,1)}, bf16[3,1024,512]{2,1,0:T(8,128)(2,1)}, u32[]{:S(2)}, u32[]{:S(2)}) %collective-permute-start.42) | collective-permute-done | bytes 3145760 | tf_op jit(solution)/shard_map/ppermute | solution.py:65
  994.9 52.5 %collective-permute-done.37 = bf16[128,2048]{1,0:T(8,128)(2,1)S(1)} collective-permute-done((bf16[128,2048]{1,0:T(8,128)(2,1)S(1)}, bf16[128,2048]{1,0:T(8,128)(2,1)S(1)}, u32[]{:S(2)}, u32[]{:S(2)}) %collective-permute-start.37) | collective-permute-done | bytes 524320 | tf_op jit(solution)/shard_map/ppermute | solution.py:54
  1048.9 42.4 %collective-permute-done.36 = bf16[128,2048]{1,0:T(8,128)(2,1)S(1)} collective-permute-done((bf16[128,2048]{1,0:T(8,128)(2,1)S(1)}, bf16[128,2048]{1,0:T(8,128)(2,1)S(1)}, u32[]{:S(2)}, u32[]{:S(2)}) %collective-permute-start.36) | collective-permute-done | bytes 524320 | tf_op jit(solution)/shard_map/ppermute | solution.py:54
  1100.9 20.4 %all-to-all-start.2 = ((bf16[4,1024,128]{2,0,1:T(4,128)(2,1)}), bf16[4,1024,128]{2,0,1:T(4,128)(2,1)S(1)}, u32[]{:S(2)}, u32[]{:S(2)}) async-start(bf16[4,1024,128]{2,0,1:T(4,128)(2,1)} %copy.371), calls=%async_computation.2 | async-start | bytes 2097152 | tf_op jit(solution)/shard_map/all_to_all | solution.py:100
  1158.8 40.1 %psum.7 = f32[]{:T(128)} all-reduce(f32[]{:T(128)S(6)} %add.425), channel_id=1, replica_groups=mesh['fsdp'=2,'ctx'=4,'tp'=4] {'fsdp','ctx','tp'}, use_global_device_ids=true, to_apply=%region_15.16 | all-reduce | flops 1 | bytes 8 | tf_op jit(solution)/shard_map/psum | solution.py:248
  (390 shorter events, 452.2 us)
Async XLA Ops:
  171.8 213.8 %all-to-all-start.1 = ((bf16[3,256,2048]{1,0,2:T(4,128)(2,1)}), bf16[3,256,2048]{1,0,2:T(4,128)(2,1)}, u32[]{:S(2)}, u32[]{:S(2)}) async-start(bf16[3,256,2048]{1,0,2:T(4,128)(2,1)} %pad_maximum_fusion.4), calls=%async_computation.1 | async-start | bytes 8388608 | tf_op jit(solution)/shard_map/all_to_all | solution.py:83
  177.0 944.3 %all-gather.3.cloned.1.call-start = ((), (), s32[]{:S(2)}) async-start(), calls=%async_computation.4 | async-start | bytes 2621440 | tf_op jit(solution)/shard_map/all_gather | solution.py:212
  180.3 81.0 %collective-permute-start.10 = (bf16[128,2048]{1,0:T(8,128)(2,1)S(1)}, bf16[128,2048]{1,0:T(8,128)(2,1)S(1)}, u32[]{:S(2)}, u32[]{:S(2)}) collective-permute-start(bf16[128,2048]{1,0:T(8,128)(2,1)S(1)} %get-tuple-element.88), channel_id=1, source_target_pairs={{0,4},{4,8},{8,12},{12,0},{1,5},{5,9},{9,13},{13,1},{2,6},{6,10},{... | collective-permute-start | bytes 1572872 | tf_op jit(solution)/shard_map/ppermute | solution.py:54
  182.4 145.3 %collective-permute-start.9 = (bf16[128,2048]{1,0:T(8,128)(2,1)S(1)}, bf16[128,2048]{1,0:T(8,128)(2,1)S(1)}, u32[]{:S(2)}, u32[]{:S(2)}) collective-permute-start(bf16[128,2048]{1,0:T(8,128)(2,1)S(1)} %get-tuple-element.89), channel_id=1, source_target_pairs={{0,8},{4,12},{8,0},{12,4},{1,9},{5,13},{9,1},{13,5},{2,10},{6,14},... | collective-permute-start | bytes 1572872 | tf_op jit(solution)/shard_map/ppermute | solution.py:54
  184.8 143.0 %collective-permute-start.8 = (bf16[128,2048]{1,0:T(8,128)(2,1)S(1)}, bf16[128,2048]{1,0:T(8,128)(2,1)S(1)}, u32[]{:S(2)}, u32[]{:S(2)}) collective-permute-start(bf16[128,2048]{1,0:T(8,128)(2,1)S(1)} %get-tuple-element.87), channel_id=1, source_target_pairs={{0,12},{4,0},{8,4},{12,8},{1,13},{5,1},{9,5},{13,9},{2,14},{6,2},{... | collective-permute-start | bytes 1572872 | tf_op jit(solution)/shard_map/ppermute | solution.py:54
  187.6 155.2 %collective-permute-start.24 = (bf16[128,2048]{1,0:T(8,128)(2,1)S(1)}, bf16[128,2048]{1,0:T(8,128)(2,1)S(1)}, u32[]{:S(2)}, u32[]{:S(2)}) collective-permute-start(bf16[128,2048]{1,0:T(8,128)(2,1)S(1)} %get-tuple-element.108), channel_id=1, source_target_pairs={{0,12},{4,0},{8,4},{12,8},{1,13},{5,1},{9,5},{13,9},{2,14},{6,2},{... | collective-permute-start | bytes 1572872 | tf_op jit(solution)/shard_map/ppermute | solution.py:54
  188.2 195.7 %collective-permute-start.23 = (bf16[128,2048]{1,0:T(8,128)(2,1)S(1)}, bf16[128,2048]{1,0:T(8,128)(2,1)S(1)}, u32[]{:S(2)}, u32[]{:S(2)}) collective-permute-start(bf16[128,2048]{1,0:T(8,128)(2,1)S(1)} %get-tuple-element.108), channel_id=1, source_target_pairs={{0,8},{4,12},{8,0},{12,4},{1,9},{5,13},{9,1},{13,5},{2,10},{6,14},... | collective-permute-start | bytes 1572872 | tf_op jit(solution)/shard_map/ppermute | solution.py:54
  261.3 122.6 %collective-permute-start.22 = (bf16[128,2048]{1,0:T(8,128)(2,1)S(1)}, bf16[128,2048]{1,0:T(8,128)(2,1)S(1)}, u32[]{:S(2)}, u32[]{:S(2)}) collective-permute-start(bf16[128,2048]{1,0:T(8,128)(2,1)S(1)} %get-tuple-element.108), channel_id=1, source_target_pairs={{0,4},{4,8},{8,12},{12,0},{1,5},{5,9},{9,13},{13,1},{2,6},{6,10},{... | collective-permute-start | bytes 1572872 | tf_op jit(solution)/shard_map/ppermute | solution.py:54
  329.5 66.8 %collective-permute-start.13 = (bf16[128,2048]{1,0:T(8,128)(2,1)}, bf16[128,2048]{1,0:T(8,128)(2,1)}, u32[]{:S(2)}, u32[]{:S(2)}) collective-permute-start(bf16[128,2048]{1,0:T(8,128)(2,1)} %fusion.76), channel_id=1, source_target_pairs={{0,12},{4,0},{8,4},{12,8},{1,13},{5,1},{9,5},{13,9},{2,14},{6,2},{... | collective-permute-start | bytes 1572872 | tf_op jit(solution)/shard_map/ppermute | solution.py:54
  394.7 72.2 %collective-permute-start.17 = (bf16[3,1024,512]{2,1,0:T(8,128)(2,1)}, bf16[3,1024,512]{2,1,0:T(8,128)(2,1)}, u32[]{:S(2)}, u32[]{:S(2)}) collective-permute-start(bf16[3,1024,512]{2,1,0:T(8,128)(2,1)} %bitcast.499), channel_id=1, source_target_pairs={{0,18},{1,19},{2,16},{3,17},{16,2},{17,3},{18,0},{19,1},{4,22},{5,... | collective-permute-start | bytes 9437192 | tf_op jit(solution)/shard_map/ppermute | solution.py:65
  396.3 137.5 %collective-permute-start.16 = (bf16[3,1024,512]{2,1,0:T(8,128)(2,1)}, bf16[3,1024,512]{2,1,0:T(8,128)(2,1)}, u32[]{:S(2)}, u32[]{:S(2)}) collective-permute-start(bf16[3,1024,512]{2,1,0:T(8,128)(2,1)} %bitcast.500), channel_id=1, source_target_pairs={{0,2},{1,3},{2,0},{3,1},{16,18},{17,19},{18,16},{19,17},{4,6},{5,7... | collective-permute-start | bytes 9437192 | tf_op jit(solution)/shard_map/ppermute | solution.py:65
  405.8 128.1 %collective-permute-start.15 = (bf16[3,1024,512]{2,1,0:T(8,128)(2,1)}, bf16[3,1024,512]{2,1,0:T(8,128)(2,1)}, u32[]{:S(2)}, u32[]{:S(2)}) collective-permute-start(bf16[3,1024,512]{2,1,0:T(8,128)(2,1)} %bitcast.501), channel_id=1, source_target_pairs={{0,16},{1,17},{2,18},{3,19},{16,0},{17,1},{18,2},{19,3},{4,20},{5,... | collective-permute-start | bytes 9437192 | tf_op jit(solution)/shard_map/ppermute | solution.py:65
  648.2 77.9 %collective-permute-start.20 = (bf16[128,2048]{1,0:T(8,128)(2,1)S(1)}, bf16[128,2048]{1,0:T(8,128)(2,1)S(1)}, u32[]{:S(2)}, u32[]{:S(2)}) collective-permute-start(bf16[128,2048]{1,0:T(8,128)(2,1)S(1)} %get-tuple-element.84), channel_id=1, source_target_pairs={{0,8},{4,12},{8,0},{12,4},{1,9},{5,13},{9,1},{13,5},{2,10},{6,14},... | collective-permute-start | bytes 1572872 | tf_op jit(solution)/shard_map/ppermute | solution.py:54
  659.7 66.4 %collective-permute-start.19 = (bf16[128,2048]{1,0:T(8,128)(2,1)S(1)}, bf16[128,2048]{1,0:T(8,128)(2,1)S(1)}, u32[]{:S(2)}, u32[]{:S(2)}) collective-permute-start(bf16[128,2048]{1,0:T(8,128)(2,1)S(1)} %get-tuple-element.82), channel_id=1, source_target_pairs={{0,12},{4,0},{8,4},{12,8},{1,13},{5,1},{9,5},{13,9},{2,14},{6,2},{... | collective-permute-start | bytes 1572872 | tf_op jit(solution)/shard_map/ppermute | solution.py:54
  795.9 72.2 %collective-permute-start.43 = (bf16[3,1024,512]{2,1,0:T(8,128)(2,1)}, bf16[3,1024,512]{2,1,0:T(8,128)(2,1)}, u32[]{:S(2)}, u32[]{:S(2)}) collective-permute-start(bf16[3,1024,512]{2,1,0:T(8,128)(2,1)} %get-tuple-element.51), channel_id=1, source_target_pairs={{0,18},{1,19},{2,16},{3,17},{16,2},{17,3},{18,0},{19,1},{4,22},{5,... | collective-permute-start | bytes 9437192 | tf_op jit(solution)/shard_map/ppermute | solution.py:65
  797.6 148.7 %collective-permute-start.42 = (bf16[3,1024,512]{2,1,0:T(8,128)(2,1)}, bf16[3,1024,512]{2,1,0:T(8,128)(2,1)}, u32[]{:S(2)}, u32[]{:S(2)}) collective-permute-start(bf16[3,1024,512]{2,1,0:T(8,128)(2,1)} %get-tuple-element.52), channel_id=1, source_target_pairs={{0,2},{1,3},{2,0},{3,1},{16,18},{17,19},{18,16},{19,17},{4,6},{5,7... | collective-permute-start | bytes 9437192 | tf_op jit(solution)/shard_map/ppermute | solution.py:65
  798.9 147.4 %collective-permute-start.41 = (bf16[3,1024,512]{2,1,0:T(8,128)(2,1)}, bf16[3,1024,512]{2,1,0:T(8,128)(2,1)}, u32[]{:S(2)}, u32[]{:S(2)}) collective-permute-start(bf16[3,1024,512]{2,1,0:T(8,128)(2,1)} %get-tuple-element.50), channel_id=1, source_target_pairs={{0,16},{1,17},{2,18},{3,19},{16,0},{17,1},{18,2},{19,3},{4,20},{5,... | collective-permute-start | bytes 9437192 | tf_op jit(solution)/shard_map/ppermute | solution.py:65
  845.0 135.0 %collective-permute-start.34 = (bf16[4,128,2048]{2,1,0:T(8,128)(2,1)}, bf16[4,128,2048]{2,1,0:T(8,128)(2,1)}, u32[]{:S(2)}, u32[]{:S(2)}) collective-permute-start(bf16[4,128,2048]{2,1,0:T(8,128)(2,1)} %slice_bitcast_fusion.14), channel_id=1, source_target_pairs={{0,1},{1,0},{2,3},{3,2},{4,5},{5,4},{6,7},{7,6},{8,9},{9,8},{10,11... | collective-permute-start | bytes 6291464 | tf_op jit(solution)/shard_map/ppermute | solution.py:57
  958.2 142.7 %all-to-all-start.3 = ((bf16[3,1024,512]{2,0,1:T(4,128)(2,1)}), bf16[3,1024,512]{2,0,1:T(4,128)(2,1)}, u32[]{:S(2)}, u32[]{:S(2)}) async-start(bf16[3,1024,512]{2,0,1:T(4,128)(2,1)} %copy.377), calls=%async_computation.3 | async-start | bytes 8388608 | tf_op jit(solution)/shard_map/all_to_all | solution.py:100
  963.1 263.3 %all-gather.5.cloned.1.call-start = ((), (), s32[]{:S(2)}) async-start(), calls=%async_computation.5 | async-start | bytes 5242880 | tf_op jit(solution)/shard_map/all_gather | solution.py:242
  985.3 105.9 %collective-permute-start.36 = (bf16[128,2048]{1,0:T(8,128)(2,1)S(1)}, bf16[128,2048]{1,0:T(8,128)(2,1)S(1)}, u32[]{:S(2)}, u32[]{:S(2)}) collective-permute-start(bf16[128,2048]{1,0:T(8,128)(2,1)S(1)} %get-tuple-element.72), channel_id=1, source_target_pairs={{0,8},{4,12},{8,0},{12,4},{1,9},{5,13},{9,1},{13,5},{2,10},{6,14},... | collective-permute-start | bytes 1572872 | tf_op jit(solution)/shard_map/ppermute | solution.py:54
  987.7 103.6 %collective-permute-start.35 = (bf16[128,2048]{1,0:T(8,128)(2,1)S(1)}, bf16[128,2048]{1,0:T(8,128)(2,1)S(1)}, u32[]{:S(2)}, u32[]{:S(2)}) collective-permute-start(bf16[128,2048]{1,0:T(8,128)(2,1)S(1)} %get-tuple-element.70), channel_id=1, source_target_pairs={{0,12},{4,0},{8,4},{12,8},{1,13},{5,1},{9,5},{13,9},{2,14},{6,2},{... | collective-permute-start | bytes 1572872 | tf_op jit(solution)/shard_map/ppermute | solution.py:54
  991.9 104.8 %collective-permute-start.40 = (bf16[4,1024,128]{2,1,0:T(8,128)(2,1)}, bf16[4,1024,128]{2,1,0:T(8,128)(2,1)}, u32[]{:S(2)}, u32[]{:S(2)}) collective-permute-start(bf16[4,1024,128]{2,1,0:T(8,128)(2,1)} %get-tuple-element.65), channel_id=1, source_target_pairs={{0,18},{1,19},{2,16},{3,17},{16,2},{17,3},{18,0},{19,1},{4,22},{5,... | collective-permute-start | bytes 3145736 | tf_op jit(solution)/shard_map/ppermute | solution.py:65
  993.6 103.2 %collective-permute-start.39 = (bf16[4,1024,128]{2,1,0:T(8,128)(2,1)}, bf16[4,1024,128]{2,1,0:T(8,128)(2,1)}, u32[]{:S(2)}, u32[]{:S(2)}) collective-permute-start(bf16[4,1024,128]{2,1,0:T(8,128)(2,1)} %get-tuple-element.66), channel_id=1, source_target_pairs={{0,2},{1,3},{2,0},{3,1},{16,18},{17,19},{18,16},{19,17},{4,6},{5,7... | collective-permute-start | bytes 3145736 | tf_op jit(solution)/shard_map/ppermute | solution.py:65
  (105 other events, 2941.7 us)
Sparse Core Ops, SparseCore 0:
  812.9 78.6 all-gather.2
  1093.7 43.1 all-gather.4
where the time goes:
time: 1250 us; the launch traced here: 1240 us
  waiting for transfers between devices  598 us (48%)
  starting transfers between devices  175 us (14%)
  local copies, waits for them, and re-layouts  154 us (12%)
  other arithmetic  139 us (11%)
  matrix products  114 us (9%)
  blocking collectives  40.1 us (3%)
  between operations  19.1 us (2%)
    ppermute x24, waiting for transfers between devices, by_ctx(): lax.ppermute(block, 'ctx', [(i, (i + shift) % n_c) for i in range(n_c)])  370 us
    ppermute x12, waiting for transfers between devices, by_pack(): return lax.ppermute(block, ('fsdp', 'tp'), pairs)  222 us
    ppermute x24, starting transfers between devices, by_ctx(): lax.ppermute(block, 'ctx', [(i, (i + shift) % n_c) for i in range(n_c)])  125 us
    dot_general x21, matrix products, dot(): lax.dot_general(left, right, (dims, ((), ())), preferred_element_type=F32)  95.9 us
    psum x1, blocking collectives, shards(): lax.psum(jnp.sum(att_total * att_total) + jnp.sum(ff_total * ff_total), (...  40.1 us
    dot_general x6, local copies, waits for them, and re-layouts, dot(): lax.dot_general(left, right, (dims, ((), ())), preferred_element_type=F32)  35.6 us
    unnamed x169, local copies, waits for them, and re-layouts  31.6 us
    all_to_all x2, starting transfers between devices, scatter_grad(): return lax.all_to_all(total.astype(BF), 'ctx', 1, 2, tiled=True).astype(F32)  25.3 us
  transfers between devices with their start and end apart: 50, of which 22 were waited for; matrix products, arithmetic and copies ran while one was open for 22% of the time, Pallas kernels for 0%

commit v1 on v0

--- a/solution.py
+++ b/solution.py
@@ -16,6 +16,29 @@
 F32 = jnp.float32
 
 
+def split_up(x, dim, size):
+    lengths = x.shape
+    pieces = x.reshape(*lengths[:dim], size, lengths[dim] // size, *lengths[dim + 1 :])
+    return jnp.moveaxis(pieces, dim, 0)
+
+
+def laid_out(pieces, dim):
+    shape = list(pieces.shape[1:])
+    shape[dim] *= pieces.shape[0]
+    return jnp.moveaxis(pieces, 0, dim).reshape(shape)
+
+
+def pairwise_exchange(x, axis, split_dim, concat_dim):
+    peers, index = (lax.axis_size(axis), lax.axis_index(axis))
+    blocks = split_up(x, split_dim, peers)
+    finished = [blocks[index]]
+    for step in range(1, peers):
+        sent = blocks[index ^ step]
+        finished.append(lax.ppermute(sent, axis, [(i, i ^ step) for i in range(peers)]))
+    blocks = jnp.stack(finished)[index ^ jnp.arange(peers)]
+    return laid_out(blocks, concat_dim)
+
+
 def mean_spread(values):
     centre = values - jnp.mean(values, axis=-1, keepdims=True)
     spread = jnp.mean(centre * centre, axis=-1, keepdims=True)
@@ -80,7 +103,7 @@
         return total
 
     def gather_weight(shard):
-        swapped = lax.all_to_all(shard.astype(BF), "ctx", 2, 1, tiled=True)
+        swapped = pairwise_exchange(shard.astype(BF), "ctx", 2, 1)
         columns = []
         for other in range(2):
             parts = [

time: 1250 us -> 1190 us (0.952)
  starting transfers between devices: 175 us -> 133 us
  waiting for transfers between devices: 598 us -> 566 us
  local copies, waits for them, and re-layouts: 154 us -> 171 us
    ppermute x24, waiting for transfers between devices: 370 us -> 293 us  [by_ctx(): lax.ppermute(block, 'ctx', [(i, (i + shift) % n_c) for i in range(n_c)])]
    ppermute x24, starting transfers between devices: 125 us -> 50.3 us  [by_ctx(): lax.ppermute(block, 'ctx', [(i, (i + shift) % n_c) for i in range(n_c)])]
    ppermute x0 -> x6, waiting for transfers between devices: none -> 54.8 us  [pairwise_exchange(): lax.ppermute(sent, axis, [(i, i ^ step) for i in range(peers)])]
    ppermute x0 -> x6, starting transfers between devices: none -> 41.6 us  [pairwise_exchange(): lax.ppermute(sent, axis, [(i, i ^ step) for i in range(peers)])]
    unnamed x169 -> x192, local copies, waits for them, and re-layouts: 31.6 us -> 41 us
    another operation x2 -> x10, local copies, waits for them, and re-layouts: 19 us -> 26 us
    dot_general x6 -> x10, local copies, waits for them, and re-layouts: 35.6 us -> 41.6 us  [dot(): lax.dot_general(left, right, (dims, ((), ())), preferred_element_type=F32)]
  transfers between devices with their start and end apart: 50 -> 54, of which waited for: 22 -> 23; matrix products, arithmetic and copies ran while one was open for 22% -> 25% of each run, Pallas kernels for 0% -> 0%
where the time goes in v1:
time: 1190 us
  waiting for transfers between devices  566 us (48%)
  local copies, waits for them, and re-layouts  171 us (14%)
  other arithmetic  140 us (12%)
  starting transfers between devices  133 us (11%)
  matrix products  119 us (10%)
  blocking collectives  40.1 us (3%)
  between operations  19.2 us (2%)
    ppermute x24, waiting for transfers between devices, by_ctx(): lax.ppermute(block, 'ctx', [(i, (i + shift) % n_c) for i in range(n_c)])  293 us
    ppermute x12, waiting for transfers between devices, by_pack(): return lax.ppermute(block, ('fsdp', 'tp'), pairs)  218 us
    dot_general x21, matrix products, dot(): lax.dot_general(left, right, (dims, ((), ())), preferred_element_type=F32)  102 us
    ppermute x6, waiting for transfers between devices, pairwise_exchange(): lax.ppermute(sent, axis, [(i, i ^ step) for i in range(peers)])  54.8 us
    ppermute x24, starting transfers between devices, by_ctx(): lax.ppermute(block, 'ctx', [(i, (i + shift) % n_c) for i in range(n_c)])  50.3 us
    dot_general x10, local copies, waits for them, and re-layouts, dot(): lax.dot_general(left, right, (dims, ((), ())), preferred_element_type=F32)  41.6 us
    ppermute x6, starting transfers between devices, pairwise_exchange(): lax.ppermute(sent, axis, [(i, i ^ step) for i in range(peers)])  41.6 us
    unnamed x192, local copies, waits for them, and re-layouts  41 us
  transfers between devices with their start and end apart: 54, of which 23 were waited for; matrix products, arithmetic and copies ran while one was open for 25% of the time, Pallas kernels for 0%

profile of v1, /device:TPU:0, one launch (start us, length us, event | category | flops | bytes accessed | tf_op | source)
XLA Modules:
  0.0 1186.6 jit_solution(6641780499520910830)
XLA Ops:
  28.0 33.1 %collective-permute-start.4 = (bf16[4,256,128]{2,1,0:T(8,128)(2,1)S(1)}, bf16[4,256,128]{2,1,0:T(8,128)(2,1)S(1)}, u32[]{:S(2)}, u32[]{:S(2)}) collective-permute-start(bf16[4,256,128]{2,1,0:T(8,128)(2,1)S(1)} %bitcast.562), channel_id=1, source_target_pairs={{0,4},{4,0},{8,12},{12,8},{1,5},{5,1},{9,13},{13,9},{2,6},{6,2},{1... | collective-permute-start | bytes 786440 | tf_op jit(solution)/shard_map/ppermute | solution.py:37
  61.1 11.8 collective-permute-done.1
  91.4 19.5 %collective-permute-done.9 = bf16[4,1024,128]{2,1,0:T(8,128)(2,1)S(1)} collective-permute-done((bf16[4,1024,128]{2,1,0:T(8,128)(2,1)S(1)}, bf16[4,1024,128]{2,1,0:T(8,128)(2,1)S(1)}, u32[]{:S(2)}, u32[]{:S(2)}) %collective-permute-start.9) | collective-permute-done | bytes 1048608 | tf_op jit(solution)/shard_map/ppermute | solution.py:88
  110.9 20.5 %collective-permute-done.8 = bf16[4,1024,128]{2,1,0:T(8,128)(2,1)} collective-permute-done((bf16[4,1024,128]{2,1,0:T(8,128)(2,1)S(1)}, bf16[4,1024,128]{2,1,0:T(8,128)(2,1)}, u32[]{:S(2)}, u32[]{:S(2)}) %collective-permute-start.8) | collective-permute-done | bytes 1048608 | tf_op jit(solution)/shard_map/ppermute | solution.py:88
  202.4 52.3 %collective-permute-done.29 = bf16[128,2048]{1,0:T(8,128)(2,1)} collective-permute-done((bf16[128,2048]{1,0:T(8,128)(2,1)}, bf16[128,2048]{1,0:T(8,128)(2,1)}, u32[]{:S(2)}, u32[]{:S(2)}) %collective-permute-start.29) | collective-permute-done | bytes 524320 | tf_op jit(solution)/shard_map/ppermute | solution.py:77
  262.3 48.6 %collective-permute-done.19 = bf16[3,256,512]{2,1,0:T(8,128)(2,1)S(1)} collective-permute-done((bf16[3,256,512]{2,1,0:T(8,128)(2,1)}, bf16[3,256,512]{2,1,0:T(8,128)(2,1)S(1)}, u32[]{:S(2)}, u32[]{:S(2)}) %collective-permute-start.19) | collective-permute-done | bytes 786464 | tf_op jit(solution)/shard_map/ppermute | solution.py:37
  340.9 12.4 %collective-permute-done.16 = bf16[128,2048]{1,0:T(8,128)(2,1)S(1)} collective-permute-done((bf16[128,2048]{1,0:T(8,128)(2,1)S(1)}, bf16[128,2048]{1,0:T(8,128)(2,1)S(1)}, u32[]{:S(2)}, u32[]{:S(2)}) %collective-permute-start.16) | collective-permute-done | bytes 524320 | tf_op jit(solution)/shard_map/ppermute | solution.py:77
  366.7 11.2 copy.317
  394.0 67.0 %collective-permute-done.22 = bf16[3,1024,512]{2,1,0:T(8,128)(2,1)} collective-permute-done((bf16[3,1024,512]{2,1,0:T(8,128)(2,1)}, bf16[3,1024,512]{2,1,0:T(8,128)(2,1)}, u32[]{:S(2)}, u32[]{:S(2)}) %collective-permute-start.22) | collective-permute-done | bytes 3145760 | tf_op jit(solution)/shard_map/ppermute | solution.py:88
  461.0 14.6 %maximum_maximum_fusion = bf16[3,2048,1024]{2,1,0:T(8,128)(2,1)S(1)} fusion(bf16[3,1024,512]{2,1,0:T(8,128)(2,1)} %collective-permute-done.23, bf16[3,1024,512]{2,1,0:T(8,128)(2,1)} %collective-permute-done.22, bf16[3,1024,512]{2,1,0:T(8,128)(2,1)} %collective-permute-done.21, bf16[3,1024,512]{2,1,0:T(8,128)(2,1)} %bitcast.71), kind=kLoop, calls=%fused_computation.4 | loop fusion | flops 50331648 | bytes 25165824 | tf_op jit(solution)/shard_map/concatenate | solution.py:113
  503.7 11.1 fusion.12
  535.0 13.9 %fusion.20 = f32[1024,2048]{1,0:T(8,128)} fusion(bf16[3,2048,1024]{2,1,0:T(8,128)(2,1)} %copy-done.14, f32[1024,1024]{1,0:T(8,128)S(1)} %copy-done.35, f32[1024,1024]{1,0:T(8,128)S(1)} %copy-done.31, f32[1024,1024]{1,0:T(8,128)} %copy.273), kind=kOutput, calls=%fused_computation.66 | convolution fusion | flops 4305453056 | bytes 25165824 | tf_op jit(solution)/shard_map/dot_general | solution.py:58
  549.0 11.6 add_convert_fusion.1
  607.9 19.3 %collective-permute-done.34 = bf16[128,2048]{1,0:T(8,128)(2,1)} collective-permute-done((bf16[128,2048]{1,0:T(8,128)(2,1)}, bf16[128,2048]{1,0:T(8,128)(2,1)}, u32[]{:S(2)}, u32[]{:S(2)}) %collective-permute-start.34) | collective-permute-done | bytes 524320 | tf_op jit(solution)/shard_map/ppermute | solution.py:77
  638.3 33.1 %collective-permute-done.26 = bf16[128,2048]{1,0:T(8,128)(2,1)S(1)} collective-permute-done((bf16[128,2048]{1,0:T(8,128)(2,1)S(1)}, bf16[128,2048]{1,0:T(8,128)(2,1)S(1)}, u32[]{:S(2)}, u32[]{:S(2)}) %collective-permute-start.26) | collective-permute-done | bytes 524320 | tf_op jit(solution)/shard_map/ppermute | solution.py:77
  672.2 10.9 collective-permute-start.38
  696.1 34.9 %collective-permute-done.37 = bf16[128,2048]{1,0:T(8,128)(2,1)S(1)} collective-permute-done((bf16[128,2048]{1,0:T(8,128)(2,1)S(1)}, bf16[128,2048]{1,0:T(8,128)(2,1)S(1)}, u32[]{:S(2)}, u32[]{:S(2)}) %collective-permute-start.37) | collective-permute-done | bytes 524320 | tf_op jit(solution)/shard_map/ppermute | solution.py:77
  746.2 12.4 %pad_maximum_fusion = f32[3,2,1024,2,512]{4,2,3,1,0:T(8,128)} fusion(f32[1,2,1024,2,512]{4,2,3,1,0:T(8,128)} %convolution_bitcast_fusion, f32[1,2,1024,2,512]{4,2,3,1,0:T(8,128)S(1)} %convolution_bitcast_fusion.1, f32[1,2,1024,2,512]{4,2,3,1,0:T(8,128)S(1)} %convolution_bitcast_fusion.2), kind=kLoop, calls=%fused_computation.3 | loop fusion | flops 12582912 | bytes 50331648 | tf_op jit(solution)/shard_map/stack | solution.py:236
  787.5 27.3 %collective-permute-done.49 = bf16[3,1024,512]{2,1,0:T(8,128)(2,1)} collective-permute-done((bf16[3,1024,512]{2,1,0:T(8,128)(2,1)}, bf16[3,1024,512]{2,1,0:T(8,128)(2,1)}, u32[]{:S(2)}, u32[]{:S(2)}) %collective-permute-start.49) | collective-permute-done | bytes 3145760 | tf_op jit(solution)/shard_map/ppermute | solution.py:88
  814.9 78.2 %collective-permute-done.48 = bf16[3,1024,512]{2,1,0:T(8,128)(2,1)} collective-permute-done((bf16[3,1024,512]{2,1,0:T(8,128)(2,1)}, bf16[3,1024,512]{2,1,0:T(8,128)(2,1)}, u32[]{:S(2)}, u32[]{:S(2)}) %collective-permute-start.48) | collective-permute-done | bytes 3145760 | tf_op jit(solution)/shard_map/ppermute | solution.py:88
  941.7 52.7 %collective-permute-done.43 = bf16[128,2048]{1,0:T(8,128)(2,1)S(1)} collective-permute-done((bf16[128,2048]{1,0:T(8,128)(2,1)S(1)}, bf16[128,2048]{1,0:T(8,128)(2,1)S(1)}, u32[]{:S(2)}, u32[]{:S(2)}) %collective-permute-start.43) | collective-permute-done | bytes 524320 | tf_op jit(solution)/shard_map/ppermute | solution.py:77
  995.9 42.4 %collective-permute-done.42 = bf16[128,2048]{1,0:T(8,128)(2,1)S(1)} collective-permute-done((bf16[128,2048]{1,0:T(8,128)(2,1)S(1)}, bf16[128,2048]{1,0:T(8,128)(2,1)S(1)}, u32[]{:S(2)}, u32[]{:S(2)}) %collective-permute-start.42) | collective-permute-done | bytes 524320 | tf_op jit(solution)/shard_map/ppermute | solution.py:77
  1047.9 20.4 %all-to-all-start = ((bf16[4,1024,128]{2,0,1:T(4,128)(2,1)}), bf16[4,1024,128]{2,0,1:T(4,128)(2,1)S(1)}, u32[]{:S(2)}, u32[]{:S(2)}) async-start(bf16[4,1024,128]{2,0,1:T(4,128)(2,1)} %copy.298), calls=%async_computation | async-start | bytes 2097152 | tf_op jit(solution)/shard_map/all_to_all | solution.py:123
  1105.8 40.1 %psum.7 = f32[]{:T(128)} all-reduce(f32[]{:T(128)S(6)} %add.457), channel_id=1, replica_groups=mesh['fsdp'=2,'ctx'=4,'tp'=4] {'fsdp','ctx','tp'}, use_global_device_ids=true, to_apply=%region_15.16 | all-reduce | flops 1 | bytes 8 | tf_op jit(solution)/shard_map/psum | solution.py:271
  (431 shorter events, 468.2 us)
Async XLA Ops:
  7.2 1061.1 %all-gather.3.cloned.1.call-start = ((), (), s32[]{:S(2)}) async-start(), calls=%async_computation.2 | async-start | bytes 2621440 | tf_op jit(solution)/shard_map/all_gather | solution.py:235
  175.6 79.1 %collective-permute-start.29 = (bf16[128,2048]{1,0:T(8,128)(2,1)}, bf16[128,2048]{1,0:T(8,128)(2,1)}, u32[]{:S(2)}, u32[]{:S(2)}) collective-permute-start(bf16[128,2048]{1,0:T(8,128)(2,1)} %get-tuple-element.116), channel_id=1, source_target_pairs={{0,8},{4,12},{8,0},{12,4},{1,9},{5,13},{9,1},{13,5},{2,10},{6,14},... | collective-permute-start | bytes 1572872 | tf_op jit(solution)/shard_map/ppermute | solution.py:77
  175.6 79.1 %collective-permute-start.28 = (bf16[128,2048]{1,0:T(8,128)(2,1)}, bf16[128,2048]{1,0:T(8,128)(2,1)}, u32[]{:S(2)}, u32[]{:S(2)}) collective-permute-start(bf16[128,2048]{1,0:T(8,128)(2,1)} %get-tuple-element.116), channel_id=1, source_target_pairs={{0,4},{4,8},{8,12},{12,0},{1,5},{5,9},{9,13},{13,1},{2,6},{6,10},{... | collective-permute-start | bytes 1572872 | tf_op jit(solution)/shard_map/ppermute | solution.py:77
  187.8 70.4 %collective-permute-start.20 = (bf16[3,256,512]{2,1,0:T(8,128)(2,1)}, bf16[3,256,512]{2,1,0:T(8,128)(2,1)}, u32[]{:S(2)}, u32[]{:S(2)}) collective-permute-start(bf16[3,256,512]{2,1,0:T(8,128)(2,1)} %bitcast.68), channel_id=1, source_target_pairs={{0,12},{4,8},{8,4},{12,0},{1,13},{5,9},{9,5},{13,1},{2,14},{6,10},... | collective-permute-start | bytes 2359304 | tf_op jit(solution)/shard_map/ppermute | solution.py:37
  194.8 116.1 %collective-permute-start.19 = (bf16[3,256,512]{2,1,0:T(8,128)(2,1)}, bf16[3,256,512]{2,1,0:T(8,128)(2,1)S(1)}, u32[]{:S(2)}, u32[]{:S(2)}) collective-permute-start(bf16[3,256,512]{2,1,0:T(8,128)(2,1)} %bitcast.552), channel_id=1, source_target_pairs={{0,8},{4,12},{8,0},{12,4},{1,9},{5,13},{9,1},{13,5},{2,10},{6,14},... | collective-permute-start | bytes 2359304 | tf_op jit(solution)/shard_map/ppermute | solution.py:37
  196.0 114.9 %collective-permute-start.18 = (bf16[3,256,512]{2,1,0:T(8,128)(2,1)}, bf16[3,256,512]{2,1,0:T(8,128)(2,1)S(1)}, u32[]{:S(2)}, u32[]{:S(2)}) collective-permute-start(bf16[3,256,512]{2,1,0:T(8,128)(2,1)} %bitcast.551), channel_id=1, source_target_pairs={{0,4},{4,0},{8,12},{12,8},{1,5},{5,1},{9,13},{13,9},{2,6},{6,2},{1... | collective-permute-start | bytes 2359304 | tf_op jit(solution)/shard_map/ppermute | solution.py:37
  254.7 68.8 %collective-permute-start.13 = (bf16[128,2048]{1,0:T(8,128)(2,1)}, bf16[128,2048]{1,0:T(8,128)(2,1)S(1)}, u32[]{:S(2)}, u32[]{:S(2)}) collective-permute-start(bf16[128,2048]{1,0:T(8,128)(2,1)} %get-tuple-element.92), channel_id=1, source_target_pairs={{0,4},{4,8},{8,12},{12,0},{1,5},{5,9},{9,13},{13,1},{2,6},{6,10},{... | collective-permute-start | bytes 1572872 | tf_op jit(solution)/shard_map/ppermute | solution.py:77
  254.7 70.1 %collective-permute-start.12 = (bf16[128,2048]{1,0:T(8,128)(2,1)}, bf16[128,2048]{1,0:T(8,128)(2,1)S(1)}, u32[]{:S(2)}, u32[]{:S(2)}) collective-permute-start(bf16[128,2048]{1,0:T(8,128)(2,1)} %get-tuple-element.93), channel_id=1, source_target_pairs={{0,8},{4,12},{8,0},{12,4},{1,9},{5,13},{9,1},{13,5},{2,10},{6,14},... | collective-permute-start | bytes 1572872 | tf_op jit(solution)/shard_map/ppermute | solution.py:77
  258.1 74.7 %collective-permute-start.11 = (bf16[128,2048]{1,0:T(8,128)(2,1)}, bf16[128,2048]{1,0:T(8,128)(2,1)S(1)}, u32[]{:S(2)}, u32[]{:S(2)}) collective-permute-start(bf16[128,2048]{1,0:T(8,128)(2,1)} %get-tuple-element.91), channel_id=1, source_target_pairs={{0,12},{4,0},{8,4},{12,8},{1,13},{5,1},{9,5},{13,9},{2,14},{6,2},{... | collective-permute-start | bytes 1572872 | tf_op jit(solution)/shard_map/ppermute | solution.py:77
  321.9 72.2 %collective-permute-start.23 = (bf16[3,1024,512]{2,1,0:T(8,128)(2,1)}, bf16[3,1024,512]{2,1,0:T(8,128)(2,1)}, u32[]{:S(2)}, u32[]{:S(2)}) collective-permute-start(bf16[3,1024,512]{2,1,0:T(8,128)(2,1)} %bitcast.71), channel_id=1, source_target_pairs={{0,18},{1,19},{2,16},{3,17},{16,2},{17,3},{18,0},{19,1},{4,22},{5,... | collective-permute-start | bytes 9437192 | tf_op jit(solution)/shard_map/ppermute | solution.py:88
  323.5 137.5 %collective-permute-start.22 = (bf16[3,1024,512]{2,1,0:T(8,128)(2,1)}, bf16[3,1024,512]{2,1,0:T(8,128)(2,1)}, u32[]{:S(2)}, u32[]{:S(2)}) collective-permute-start(bf16[3,1024,512]{2,1,0:T(8,128)(2,1)} %bitcast.71), channel_id=1, source_target_pairs={{0,2},{1,3},{2,0},{3,1},{16,18},{17,19},{18,16},{19,17},{4,6},{5,7... | collective-permute-start | bytes 9437192 | tf_op jit(solution)/shard_map/ppermute | solution.py:88
  324.8 136.2 %collective-permute-start.21 = (bf16[3,1024,512]{2,1,0:T(8,128)(2,1)}, bf16[3,1024,512]{2,1,0:T(8,128)(2,1)}, u32[]{:S(2)}, u32[]{:S(2)}) collective-permute-start(bf16[3,1024,512]{2,1,0:T(8,128)(2,1)} %bitcast.71), channel_id=1, source_target_pairs={{0,16},{1,17},{2,18},{3,19},{16,0},{17,1},{18,2},{19,3},{4,20},{5,... | collective-permute-start | bytes 9437192 | tf_op jit(solution)/shard_map/ppermute | solution.py:88
  388.6 103.0 %collective-permute-start.17 = (bf16[4,128,2048]{2,1,0:T(8,128)(2,1)}, bf16[4,128,2048]{2,1,0:T(8,128)(2,1)}, u32[]{:S(2)}, u32[]{:S(2)}) collective-permute-start(bf16[4,128,2048]{2,1,0:T(8,128)(2,1)} %get-tuple-element.90), channel_id=1, source_target_pairs={{0,1},{1,0},{2,3},{3,2},{4,5},{5,4},{6,7},{7,6},{8,9},{9,8},{10,11... | collective-permute-start | bytes 6291464 | tf_op jit(solution)/shard_map/ppermute | solution.py:80
  595.3 76.1 %collective-permute-start.26 = (bf16[128,2048]{1,0:T(8,128)(2,1)S(1)}, bf16[128,2048]{1,0:T(8,128)(2,1)S(1)}, u32[]{:S(2)}, u32[]{:S(2)}) collective-permute-start(bf16[128,2048]{1,0:T(8,128)(2,1)S(1)} %get-tuple-element.88), channel_id=1, source_target_pairs={{0,8},{4,12},{8,0},{12,4},{1,9},{5,13},{9,1},{13,5},{2,10},{6,14},... | collective-permute-start | bytes 1572872 | tf_op jit(solution)/shard_map/ppermute | solution.py:77
  742.7 72.2 %collective-permute-start.49 = (bf16[3,1024,512]{2,1,0:T(8,128)(2,1)}, bf16[3,1024,512]{2,1,0:T(8,128)(2,1)}, u32[]{:S(2)}, u32[]{:S(2)}) collective-permute-start(bf16[3,1024,512]{2,1,0:T(8,128)(2,1)} %get-tuple-element.51), channel_id=1, source_target_pairs={{0,18},{1,19},{2,16},{3,17},{16,2},{17,3},{18,0},{19,1},{4,22},{5,... | collective-permute-start | bytes 9437192 | tf_op jit(solution)/shard_map/ppermute | solution.py:88
  744.4 148.7 %collective-permute-start.48 = (bf16[3,1024,512]{2,1,0:T(8,128)(2,1)}, bf16[3,1024,512]{2,1,0:T(8,128)(2,1)}, u32[]{:S(2)}, u32[]{:S(2)}) collective-permute-start(bf16[3,1024,512]{2,1,0:T(8,128)(2,1)} %get-tuple-element.52), channel_id=1, source_target_pairs={{0,2},{1,3},{2,0},{3,1},{16,18},{17,19},{18,16},{19,17},{4,6},{5,7... | collective-permute-start | bytes 9437192 | tf_op jit(solution)/shard_map/ppermute | solution.py:88
  745.7 147.4 %collective-permute-start.47 = (bf16[3,1024,512]{2,1,0:T(8,128)(2,1)}, bf16[3,1024,512]{2,1,0:T(8,128)(2,1)}, u32[]{:S(2)}, u32[]{:S(2)}) collective-permute-start(bf16[3,1024,512]{2,1,0:T(8,128)(2,1)} %get-tuple-element.50), channel_id=1, source_target_pairs={{0,16},{1,17},{2,18},{3,19},{16,0},{17,1},{18,2},{19,3},{4,20},{5,... | collective-permute-start | bytes 9437192 | tf_op jit(solution)/shard_map/ppermute | solution.py:88
  787.5 139.2 %collective-permute-start.40 = (bf16[4,128,2048]{2,1,0:T(8,128)(2,1)}, bf16[4,128,2048]{2,1,0:T(8,128)(2,1)}, u32[]{:S(2)}, u32[]{:S(2)}) collective-permute-start(bf16[4,128,2048]{2,1,0:T(8,128)(2,1)} %slice_bitcast_fusion.14), channel_id=1, source_target_pairs={{0,1},{1,0},{2,3},{3,2},{4,5},{5,4},{6,7},{7,6},{8,9},{9,8},{10,11... | collective-permute-start | bytes 6291464 | tf_op jit(solution)/shard_map/ppermute | solution.py:80
  905.2 142.6 %all-to-all-start.1 = ((bf16[3,1024,512]{2,0,1:T(4,128)(2,1)}), bf16[3,1024,512]{2,0,1:T(4,128)(2,1)}, u32[]{:S(2)}, u32[]{:S(2)}) async-start(bf16[3,1024,512]{2,0,1:T(4,128)(2,1)} %copy.304), calls=%async_computation.1 | async-start | bytes 8388608 | tf_op jit(solution)/shard_map/all_to_all | solution.py:123
  910.1 263.3 %all-gather.5.cloned.1.call-start = ((), (), s32[]{:S(2)}) async-start(), calls=%async_computation.3 | async-start | bytes 5242880 | tf_op jit(solution)/shard_map/all_gather | solution.py:265
  932.1 106.1 %collective-permute-start.42 = (bf16[128,2048]{1,0:T(8,128)(2,1)S(1)}, bf16[128,2048]{1,0:T(8,128)(2,1)S(1)}, u32[]{:S(2)}, u32[]{:S(2)}) collective-permute-start(bf16[128,2048]{1,0:T(8,128)(2,1)S(1)} %get-tuple-element.76), channel_id=1, source_target_pairs={{0,8},{4,12},{8,0},{12,4},{1,9},{5,13},{9,1},{13,5},{2,10},{6,14},... | collective-permute-start | bytes 1572872 | tf_op jit(solution)/shard_map/ppermute | solution.py:77
  934.5 103.8 %collective-permute-start.41 = (bf16[128,2048]{1,0:T(8,128)(2,1)S(1)}, bf16[128,2048]{1,0:T(8,128)(2,1)S(1)}, u32[]{:S(2)}, u32[]{:S(2)}) collective-permute-start(bf16[128,2048]{1,0:T(8,128)(2,1)S(1)} %get-tuple-element.74), channel_id=1, source_target_pairs={{0,12},{4,0},{8,4},{12,8},{1,13},{5,1},{9,5},{13,9},{2,14},{6,2},{... | collective-permute-start | bytes 1572872 | tf_op jit(solution)/shard_map/ppermute | solution.py:77
  938.7 105.0 %collective-permute-start.46 = (bf16[4,1024,128]{2,1,0:T(8,128)(2,1)}, bf16[4,1024,128]{2,1,0:T(8,128)(2,1)}, u32[]{:S(2)}, u32[]{:S(2)}) collective-permute-start(bf16[4,1024,128]{2,1,0:T(8,128)(2,1)} %get-tuple-element.65), channel_id=1, source_target_pairs={{0,18},{1,19},{2,16},{3,17},{16,2},{17,3},{18,0},{19,1},{4,22},{5,... | collective-permute-start | bytes 3145736 | tf_op jit(solution)/shard_map/ppermute | solution.py:88
  940.4 103.4 %collective-permute-start.45 = (bf16[4,1024,128]{2,1,0:T(8,128)(2,1)}, bf16[4,1024,128]{2,1,0:T(8,128)(2,1)}, u32[]{:S(2)}, u32[]{:S(2)}) collective-permute-start(bf16[4,1024,128]{2,1,0:T(8,128)(2,1)} %get-tuple-element.66), channel_id=1, source_target_pairs={{0,2},{1,3},{2,0},{3,1},{16,18},{17,19},{18,16},{19,17},{4,6},{5,7... | collective-permute-start | bytes 3145736 | tf_op jit(solution)/shard_map/ppermute | solution.py:88
  (119 other events, 3198.7 us)
Sparse Core Ops, SparseCore 0:
  759.6 78.7 all-gather.2
  1040.7 43.1 all-gather.4
